TPU v7x, 256 devices: a whole 4x4x8 slice. The times are simulated.
256 devices in a mesh: ctx: 16 (over y, x), head: 16 (over z, core).
Axes of the slice: x: 4, y: 4, z: 8, core: 2. Of those that a mesh axis runs over, the one named last changes fastest.
Arguments:
- queries: bfloat16 [2, 4096, 8192], P(None, 'ctx', 'head'), may hold values from -4.5 to 4.5
- key_rows: bfloat16 [2, 4096, 512], P(None, 'ctx'), may hold values from -4.5 to 4.5
- value_rows: bfloat16 [2, 4096, 512], P(None, 'ctx'), may hold values from -6 to 6
- out_weight: bfloat16 [8192, 8192], P('head'), may hold values from -0.0625 to 0.0625
- span_owner: int32 [2, 16], replicated, may hold values from 0 to 15, each once within a row
- vertical_blocks: int32 [64, 4], replicated, may hold values from 0 to 63, as said below
- slash_offsets: int32 [64, 4], replicated, may hold values from 1 to 63, as said below
Outputs:
- projected: bfloat16 [2, 4096, 8192], P(None, ('ctx', 'head'))
Inputs may be any that keep to these rules, and one draw needn't show every extreme that they name: `vertical_blocks`: the 4 entries of a head are distinct block numbers. `slash_offsets`: the 4 entries of a head are distinct.
All inputs are finite; a program needn't handle non-finite values.
Results may differ from a plain program's by a relative error of at most 0.017.
Values may be sent and summed in bfloat16 or wider, within the bound.
No kernel may reach another device: no remote copies, remote signals or barrier semaphores. Data moves between devices by JAX's collectives and lax.ppermute only.
A program may use at most 64 MiB of HBM per device.

v0:
```python
import math
import jax
import jax.numpy as jnp
from jax import lax
from jax.sharding import PartitionSpec as P

QH = 64
KVH = 4
HD = 128
BLK = 128
STEPS = 2


def tile_blocks(block_ids, vertical, slanted, owner_flat, span_blocks, span_count):
    column = block_ids[:, None]
    vert_rows = jnp.broadcast_to(vertical[None, :], (block_ids.shape[0], vertical.shape[0]))
    slash_rows = column - slanted[None, :]
    vert_valid = vert_rows < column
    repeated = jnp.any(slash_rows[:, :, None] == vertical[None, None, :], axis=2)
    slash_valid = (slash_rows >= 0) & jnp.logical_not(repeated)
    chosen = jnp.concatenate([column, vert_rows, slash_rows], axis=1)
    allowed = jnp.concatenate([jnp.ones_like(column, dtype=bool), vert_valid, slash_valid], axis=1)
    chosen = jnp.where(allowed, chosen, column)
    span_index = chosen // span_blocks
    slot_ids = jnp.arange(owner_flat.shape[0], dtype=jnp.int32)
    holder = jnp.sum(
        jnp.where(span_index[:, :, None] == slot_ids[None, None, :], owner_flat[None, None, :], 0),
        axis=2,
    )
    step_index = span_index // span_count
    stored = (step_index * span_count + holder) * span_blocks + chosen % span_blocks
    return (stored, allowed)


def block_mask(allowed, block_rows):
    positions = jnp.arange(block_rows, dtype=jnp.int32)
    causal = positions[None, :] <= positions[:, None]
    tile_count = allowed.shape[1]
    first_tile = jnp.arange(tile_count, dtype=jnp.int32) == 0
    inside = causal[None, :, None, :] | jnp.logical_not(first_tile)[None, None, :, None]
    visible = allowed[:, None, :, None] & inside
    return visible.reshape(allowed.shape[0], block_rows, tile_count * block_rows)


def attend_tiles(query_tile_set, key_store, value_store, stored, allowed):
    block_count = stored.shape[0]
    tile_count = stored.shape[1]
    block_rows = query_tile_set.shape[1]
    head_features = query_tile_set.shape[2]
    key_tile_set = jnp.take(key_store, stored.reshape(-1), axis=0).reshape(
        block_count, tile_count * block_rows, head_features
    )
    value_tile_set = jnp.take(value_store, stored.reshape(-1), axis=0).reshape(
        block_count, tile_count * block_rows, head_features
    )
    logit_scores = jnp.einsum(
        "zcs,zvs->zcv", query_tile_set, key_tile_set, preferred_element_type=jnp.float32
    ) * (1.0 / math.sqrt(head_features))
    logit_scores = jnp.where(block_mask(allowed, block_rows), logit_scores, -jnp.inf)
    largest = jnp.max(logit_scores, axis=2, keepdims=True)
    weights = jnp.exp(logit_scores - largest)
    totals = jnp.sum(weights, axis=2, keepdims=True)
    mixed_output = jnp.einsum(
        "ynj,yjw->ynw",
        weights.astype(jnp.bfloat16),
        value_tile_set,
        preferred_element_type=jnp.float32,
    )
    return (mixed_output / totals).astype(jnp.bfloat16)


def local(queries, key_rows, value_rows, out_weight, span_owner, vertical_blocks, slash_offsets):
    local_heads = queries.shape[2] // HD
    span_rows = queries.shape[1]
    span_blocks = span_rows // BLK
    span_count = lax.axis_size("ctx")
    head_groups = lax.axis_size("head")
    rows_share = span_rows // head_groups
    first_head = lax.axis_index("head") * local_heads
    kv_head = first_head // (QH // KVH)
    vertical = lax.dynamic_slice_in_dim(vertical_blocks, first_head, local_heads, 0)
    slanted = lax.dynamic_slice_in_dim(slash_offsets, first_head, local_heads, 0)
    own_keys = lax.dynamic_slice_in_dim(key_rows, kv_head * HD, HD, 2)
    own_values = lax.dynamic_slice_in_dim(value_rows, kv_head * HD, HD, 2)
    paired = jnp.stack([own_keys, own_values], axis=1)
    owner_flat = span_owner.reshape(-1)
    device = lax.axis_index("ctx")
    device_ids = jnp.arange(span_count, dtype=jnp.int32)
    places = jnp.sum(device_ids[None, :] * (span_owner == device).astype(jnp.int32), axis=1)
    tiler = jax.vmap(tile_blocks, in_axes=(None, 0, 0, None, None, None))
    gathered = lax.all_gather(paired, "ctx", axis=2, tiled=True)
    outputs = []
    for current in range(STEPS):
        kv_store = gathered[: current + 1]
        key_store = kv_store[:, 0].reshape(-1, BLK, HD)
        value_store = kv_store[:, 1].reshape(-1, BLK, HD)
        block_ids = (current * span_count + places[current]) * span_blocks + jnp.arange(
            span_blocks, dtype=jnp.int32
        )
        stored, allowed = tiler(block_ids, vertical, slanted, owner_flat, span_blocks, span_count)
        stored = stored.reshape(local_heads * span_blocks, -1)
        allowed = allowed.reshape(local_heads * span_blocks, -1)
        query_tile_set = (
            queries[current]
            .reshape(span_blocks, BLK, local_heads, HD)
            .transpose(2, 0, 1, 3)
            .reshape(local_heads * span_blocks, BLK, HD)
        )
        result_tiles = attend_tiles(query_tile_set, key_store, value_store, stored, allowed)
        attended = (
            result_tiles.reshape(local_heads, span_blocks, BLK, HD)
            .transpose(1, 2, 0, 3)
            .reshape(span_rows, local_heads * HD)
        )
        outputs.append(attended)
    arranged = (
        jnp.stack(outputs)
        .reshape(STEPS, head_groups, rows_share, -1)
        .transpose(1, 0, 2, 3)
        .reshape(STEPS * span_rows, -1)
    )
    summed = lax.psum_scatter(
        jnp.dot(arranged, out_weight, preferred_element_type=jnp.float32).astype(jnp.bfloat16),
        "head",
        scatter_dimension=0,
        tiled=True,
    ).astype(jnp.float32)
    return summed.reshape(STEPS, rows_share, -1).astype(jnp.bfloat16)


def solution(mesh):
    in_specs = (
        P(None, "ctx", "head"),
        P(None, "ctx", None),
        P(None, "ctx", None),
        P("head", None),
        P(),
        P(),
        P(),
    )
    out_specs = P(None, ("ctx", "head"), None)
    return jax.shard_map(local, mesh=mesh, in_specs=in_specs, out_specs=out_specs, check_vma=False)
```

profile of v0, /device:TPU:2, one launch (start us, length us, event | category | flops | bytes accessed | tf_op | source)
XLA Modules:
  0.0 190.6 jit_solution(16768299913413299130)
XLA Ops:
  6.5 1.0 dynamic-slice_bitcast_fusion
  7.5 0.7 pad_maximum_fusion
  8.3 0.8 broadcast_in_dim_reshape.2
  9.3 0.8 fusion.26
  10.1 0.6 fusion.33
  11.9 0.8 constant_dynamic-slice_fusion.1
  12.9 0.4 compare_reduce_fusion.1
  13.6 0.1 and_select_fusion
  13.9 0.8 select_reduce_fusion.1
  15.2 1.1 fusion.31
  16.9 0.8 copy.45
  17.9 0.2 bitcast_or_fusion
  18.4 50.8 %all-gather.2.cloned.1.call-done = bf16[2,2,4096,128]{3,2,0,1:T(8,128)(2,1)} async-done(((bf16[2,2,256,128]{3,2,0,1:T(8,128)(2,1)}), bf16[2,2,4096,128]{3,2,0,1:T(8,128)(2,1)}) %all-gather.2.cloned.1.call-update) | async-done | bytes 4194320 | tf_op jit(solution)/shard_map/all_gather | solution.py:91
  69.2 3.8 %fusion.30 = (bf16[2,1,4096,128]{3,2,0,1:T(8,128)(2,1)}, bf16[2,1,4096,128]{3,2,0,1:T(8,128)(2,1)S(1)}) fusion(bf16[2,2,4096,128]{3,2,0,1:T(8,128)(2,1)} %all-gather.2.cloned.1.call-done), kind=kLoop, calls=%fused_computation.106 | loop fusion | bytes 8388608 | tf_op jit(solution)/shard_map/slice | solution.py:95
  73.0 4.0 %gather_fusion.2 = bf16[72,128,128]{2,1,0:T(8,128)(2,1)} fusion(bf16[64,128,128]{2,1,0:T(8,128)(2,1)} %bitcast.63, s32[1024]{0:T(1024)S(1)} %pad_clamp_fusion), kind=kCustom, calls=%fused_computation.1.clone | custom fusion | bytes 4718880 | tf_op jit(solution)/shard_map/jit(_take)/gather | solution.py:50
  77.1 2.5 %gather_fusion.3 = bf16[72,128,128]{2,1,0:T(8,128)(2,1)} fusion(bf16[64,128,128]{2,1,0:T(8,128)(2,1)S(1)} %bitcast.62, s32[1024]{0:T(1024)S(1)} %pad_clamp_fusion), kind=kCustom, calls=%fused_computation.3.clone | custom fusion | bytes 4718880 | tf_op jit(solution)/shard_map/jit(_take)/gather | solution.py:53
  79.5 2.9 %broadcast_select_fusion.1 = (bf16[72,128,128]{2,1,0:T(8,128)(2,1)S(1)}, bf16[72,128,128]{2,1,0:T(8,128)(2,1)S(1)}) fusion(bf16[72,128,128]{2,1,0:T(8,128)(2,1)} %gather_fusion.2, pred[72]{0:T(512)(128)(4,1)S(1)} %get-tuple-element.13, bf16[72,128,128]{2,1,0:T(8,128)(2,1)} %gather_fusion.3), kind=kLoop, calls=%fused_computation.20 | loop fusion | flops 2359296 | bytes 9437256 | tf_op jit(solution)/shard_map/jit(_take)/select_n | solution.py:50
  82.4 3.2 %fusion.34 = (f32[8,128]{1,0:T(8,128)S(1)}, f32[8,128,1152]{1,2,0:T(8,128)S(1)}) fusion(bf16[8,1152,128]{2,1,0:T(8,128)(2,1)S(1)} %bitcast.67, bf16[8,128,128]{2,1,0:T(8,128)(2,1)S(1)} %bitcast.73, pred[128,1152]{0,1:T(8,128)(4,1)S(1)} %bitcast_or_fusion, pred[8,1152]{1,0:T(8,128)(4,1)S(1)} %broadcast_bitcast_fusion), kind=kOutput, calls=%fused_computation.110 | convolution fusion | flops 306707456 | bytes 7500800 | tf_op jit(solution)/shard_map/zcs,zvs->zcv/dot_general | solution.py:56
  85.6 0.6 fusion.2
  86.2 1.3 fusion.19
  87.5 0.2 copy.63
  87.7 0.8 stack.20
  88.5 1.7 fusion.29
  90.2 2.4 %gather_fusion = bf16[72,128,128]{2,1,0:T(8,128)(2,1)} fusion(bf16[32,128,128]{2,1,0:T(8,128)(2,1)S(1)} %bitcast.61, s32[1024]{0:T(1024)S(1)} %pad_clamp_fusion.1), kind=kCustom, calls=%fused_computation.clone | custom fusion | bytes 4718880 | tf_op jit(solution)/shard_map/jit(_take)/gather | solution.py:50
  92.6 2.4 %gather_fusion.1 = bf16[72,128,128]{2,1,0:T(8,128)(2,1)} fusion(bf16[32,128,128]{2,1,0:T(8,128)(2,1)S(1)} %bitcast.60, s32[1024]{0:T(1024)S(1)} %pad_clamp_fusion.1), kind=kCustom, calls=%fused_computation.2.clone | custom fusion | bytes 4718880 | tf_op jit(solution)/shard_map/jit(_take)/gather | solution.py:53
  95.0 2.4 %broadcast_select_fusion.3 = (bf16[72,128,128]{2,1,0:T(8,128)(2,1)S(1)}, bf16[72,128,128]{2,1,0:T(8,128)(2,1)S(1)}) fusion(bf16[72,128,128]{2,1,0:T(8,128)(2,1)S(1)} %copy-done.1, pred[72]{0:T(512)(128)(4,1)S(1)} %get-tuple-element.55, bf16[72,128,128]{2,1,0:T(8,128)(2,1)} %gather_fusion.1), kind=kLoop, calls=%fused_computation.22 | loop fusion | flops 2359296 | bytes 9437256 | tf_op jit(solution)/shard_map/jit(_take)/select_n | solution.py:50
  97.5 2.9 %fusion.35 = (f32[8,128]{1,0:T(8,128)S(1)}, f32[8,128,1152]{1,2,0:T(8,128)S(1)}) fusion(bf16[8,1152,128]{2,1,0:T(8,128)(2,1)S(1)} %bitcast.66, bf16[8,128,128]{2,1,0:T(8,128)(2,1)S(1)} %bitcast.74, pred[128,1152]{0,1:T(8,128)(4,1)S(1)} %copy-done.5, pred[8,1152]{1,0:T(8,128)(4,1)S(1)} %broadcast_bitcast_fusion.1), kind=kOutput, calls=%fused_computation.111 | convolution fusion | flops 306707456 | bytes 7500800 | tf_op jit(solution)/shard_map/zcs,zvs->zcv/dot_general | solution.py:56
  100.4 0.6 fusion
  101.0 1.3 fusion.13
  102.3 0.2 copy.64
  102.7 10.2 %convolution_convert_fusion = bf16[512,8192]{1,0:T(8,128)(2,1)} fusion(bf16[512,512]{1,0:T(8,128)(2,1)S(1)} %bitcast.72, bf16[512,8192]{1,0:T(8,128)(2,1)} %param.14), kind=kOutput, calls=%fused_computation.4 | convolution fusion | flops 4299161600 | bytes 17301504 | tf_op jit(solution)/shard_map/dot_general | solution.py:123
  113.0 70.7 %reduce-scatter.2.cloned.1.call-done = bf16[32,8192]{1,0:T(8,128)(2,1)} async-done(((bf16[512,8192]{1,0:T(8,128)(2,1)}), bf16[32,8192]{1,0:T(8,128)(2,1)}) %reduce-scatter.2.cloned.1.call-update) | async-done | bytes 524304 | tf_op jit(solution)/shard_map/reduce_scatter | solution.py:122
  (60 shorter events, 2.6 us)
Async XLA Ops:
  6.5 2.6 %copy-start = (s32[64,4]{0,1:T(4,128)S(1)}, s32[64,4]{0,1:T(4,128)}, u32[]{:S(2)}) copy-start(s32[64,4]{0,1:T(4,128)} %param.17) | copy-start | bytes 3076
  6.5 62.6 %all-gather.2.cloned.1.call-start = ((), (), s32[]{:S(2)}) async-start(), calls=%async_computation.1 | async-start | bytes 4456448 | tf_op jit(solution)/shard_map/all_gather | solution.py:91
  8.3 175.4 %reduce-scatter.2.cloned.1.call-start = ((), (), s32[]{:S(2)}) async-start(), calls=%async_computation.2 | async-start | bytes 8912896 | tf_op jit(solution)/shard_map/reduce_scatter | solution.py:122
  18.1 64.3 %copy-start.4 = (pred[128,1152]{0,1:T(8,128)(4,1)}, pred[128,1152]{0,1:T(8,128)(4,1)S(1)}, u32[]{:S(2)}) copy-start(pred[128,1152]{0,1:T(8,128)(4,1)S(1)} %bitcast_or_fusion) | copy-start | bytes 442372
  92.6 2.4 %copy-start.1 = (bf16[72,128,128]{2,1,0:T(8,128)(2,1)S(1)}, bf16[72,128,128]{2,1,0:T(8,128)(2,1)}, u32[]{:S(2)}) copy-start(bf16[72,128,128]{2,1,0:T(8,128)(2,1)} %gather_fusion) | copy-start | bytes 7077892
  95.0 2.4 %copy-start.3 = (bf16[2,128,4,128]{3,1,0,2:T(8,128)(2,1)S(1)}, bf16[2,128,4,128]{3,1,0,2:T(8,128)(2,1)}, u32[]{:S(2)}) copy-start(bf16[2,128,4,128]{3,1,0,2:T(8,128)(2,1)} %copy.45) | copy-start | bytes 786436
  95.0 2.4 %copy-start.5 = (pred[128,1152]{0,1:T(8,128)(4,1)S(1)}, pred[128,1152]{0,1:T(8,128)(4,1)}, u32[]{:S(2)}) copy-start(pred[128,1152]{0,1:T(8,128)(4,1)} %copy-done.4) | copy-start | bytes 442372
  101.0 1.6 copy-start.2
Sparse Core Ops, SparseCore 0:
  9.8 59.3 all-gather.1
  113.1 70.5 reduce-scatter.1
where the time goes:
time: 191 us
  waiting for transfers between devices  122 us (64%)
  local copies, waits for them, and re-layouts  25.2 us (13%)
  matrix products  18.8 us (10%)
  between operations  14.9 us (8%)
  other arithmetic  9.99 us (5%)
    reduce_scatter x1, waiting for transfers between devices, local(): lax.psum_scatter(jnp.dot(arranged, out_weight, preferred_element_type=jnp...  70.7 us
    all_gather x1, waiting for transfers between devices, local(): gathered = lax.all_gather(paired, 'ctx', axis=2, tiled=True)  50.8 us
    dot_general x1, matrix products, local(): jnp.dot(arranged, out_weight, preferred_element_type=jnp.float32)  10.2 us
    gather x2, local copies, waits for them, and re-layouts, attend_tiles(): jnp.take(key_store, stored.reshape(-1), axis=0)  6.48 us
    dot_general x2, matrix products, attend_tiles(): jnp.einsum('zcs,zvs->zcv', query_tile_set, key_tile_set, preferred_elemen...  6.08 us
    slice x2, local copies, waits for them, and re-layouts, local(): key_store = kv_store[:, 0].reshape(-1, BLK, HD)  5.51 us
    select_n x2, other arithmetic, attend_tiles(): jnp.take(key_store, stored.reshape(-1), axis=0)  5.24 us
    gather x2, local copies, waits for them, and re-layouts, attend_tiles(): jnp.take(value_store, stored.reshape(-1), axis=0)  4.91 us
  transfers between devices with their start and end apart: 2, of which 2 were waited for; matrix products, arithmetic and copies ran while one was open for 5% of the time, Pallas kernels for 0%

commit v1 on v0

--- a/solution.py
+++ b/solution.py
@@ -88,7 +88,10 @@
     device_ids = jnp.arange(span_count, dtype=jnp.int32)
     places = jnp.sum(device_ids[None, :] * (span_owner == device).astype(jnp.int32), axis=1)
     tiler = jax.vmap(tile_blocks, in_axes=(None, 0, 0, None, None, None))
-    gathered = lax.all_gather(paired, "ctx", axis=2, tiled=True)
+    scales_work = lambda inner_x, a_name, array_dim: jnp.concatenate(
+        lax.all_to_all(jnp.stack(lax.axis_size(a_name) * [inner_x]), a_name, 0, 0), axis=array_dim
+    )
+    gathered = scales_work(paired, "ctx", 2)
     outputs = []
     for current in range(STEPS):
         kv_store = gathered[: current + 1]

time: 191 us -> 205 us (1.073)
  starting transfers between devices: 0.04 us -> 7.65 us
  waiting for transfers between devices: 122 us -> 127 us
  local copies, waits for them, and re-layouts: 25.2 us -> 27.3 us
    all_to_all x0 -> x1, waiting for transfers between devices: none -> 52.2 us  [local(): lax.all_to_all(jnp.stack(lax.axis_size(a_name) * [inner_x]), a_name, 0, 0)]
    all_gather x1 -> x0, waiting for transfers between devices: 50.8 us -> none  [local(): gathered = lax.all_gather(paired, 'ctx', axis=2, tiled=True)]
    all_to_all x0 -> x1, starting transfers between devices: none -> 7.61 us  [local(): lax.all_to_all(jnp.stack(lax.axis_size(a_name) * [inner_x]), a_name, 0, 0)]
    reduce_scatter x1, waiting for transfers between devices: 70.7 us -> 75.1 us  [local(): lax.psum_scatter(jnp.dot(arranged, out_weight, preferred_element_type=jnp...]
    slice x2, local copies, waits for them, and re-layouts: 5.51 us -> 1.94 us  [local(): key_store = kv_store[:, 0].reshape(-1, BLK, HD)]
    another operation x0 -> x1, local copies, waits for them, and re-layouts: none -> 3 us  [local(): jnp.stack(lax.axis_size(a_name) * [inner_x])]
    all_to_all x0 -> x1, local copies, waits for them, and re-layouts: none -> 2.46 us  [local(): lax.all_to_all(jnp.stack(lax.axis_size(a_name) * [inner_x]), a_name, 0, 0)]
  transfers between devices with their start and end apart: 2 -> 2, of which waited for: 2 -> 2; matrix products, arithmetic and copies ran while one was open for 5% -> 3% of each run, Pallas kernels for 0% -> 0%
where the time goes in v1:
time: 205 us
  waiting for transfers between devices  127 us (62%)
  local copies, waits for them, and re-layouts  27.3 us (13%)
  matrix products  18.8 us (9%)
  between operations  14.9 us (7%)
  other arithmetic  8.63 us (4%)
  starting transfers between devices  7.65 us (4%)
    reduce_scatter x1, waiting for transfers between devices, local(): lax.psum_scatter(jnp.dot(arranged, out_weight, preferred_element_type=jnp...  75.1 us
    all_to_all x1, waiting for transfers between devices, local(): lax.all_to_all(jnp.stack(lax.axis_size(a_name) * [inner_x]), a_name, 0, 0)  52.2 us
    dot_general x1, matrix products, local(): jnp.dot(arranged, out_weight, preferred_element_type=jnp.float32)  10.2 us
    all_to_all x1, starting transfers between devices, local(): lax.all_to_all(jnp.stack(lax.axis_size(a_name) * [inner_x]), a_name, 0, 0)  7.61 us
    gather x2, local copies, waits for them, and re-layouts, attend_tiles(): jnp.take(key_store, stored.reshape(-1), axis=0)  6.5 us
    dot_general x2, matrix products, attend_tiles(): jnp.einsum('zcs,zvs->zcv', query_tile_set, key_tile_set, preferred_elemen...  6.06 us
    select_n x2, other arithmetic, attend_tiles(): jnp.take(key_store, stored.reshape(-1), axis=0)  5.24 us
    gather x2, local copies, waits for them, and re-layouts, attend_tiles(): jnp.take(value_store, stored.reshape(-1), axis=0)  4.92 us
  transfers between devices with their start and end apart: 2, of which 2 were waited for; matrix products, arithmetic and copies ran while one was open for 3% of the time, Pallas kernels for 0%

profile of v1, /device:TPU:2, one launch (start us, length us, event | category | flops | bytes accessed | tf_op | source)
XLA Modules:
  0.0 204.6 jit_solution(4407788913346611130)
XLA Ops:
  6.5 1.0 dynamic-slice_bitcast_fusion
  7.6 3.0 %stack.17 = bf16[16,2,2,256,128]{4,3,2,1,0:T(8,128)(2,1)} broadcast(bf16[2,2,256,128]{3,2,1,0:T(8,128)(2,1)S(1)} %pad_maximum_fusion), dimensions={1,2,3,4} | broadcast | bytes 4456448 | tf_op jit(solution)/shard_map/stack | solution.py:92
  10.6 7.6 %all-to-all-start = ((bf16[16,2,2,256,128]{4,3,2,1,0:T(8,128)(2,1)}), bf16[16,2,2,256,128]{4,3,2,1,0:T(8,128)(2,1)}, u32[]{:S(2)}, u32[]{:S(2)}) async-start(bf16[16,2,2,256,128]{4,3,2,1,0:T(8,128)(2,1)} %stack.17), calls=%async_computation | async-start | bytes 8388608 | tf_op jit(solution)/shard_map/all_to_all | solution.py:92
  18.6 0.6 fusion.33
  20.7 0.4 compare_reduce_fusion.1
  21.4 0.1 and_select_fusion
  21.7 0.8 select_reduce_fusion.1
  23.7 0.8 copy.63
  24.7 0.2 bitcast_or_fusion
  25.1 52.2 %all-to-all-done = bf16[16,2,2,256,128]{4,3,2,1,0:T(8,128)(2,1)} async-done(((bf16[16,2,2,256,128]{4,3,2,1,0:T(8,128)(2,1)}), bf16[16,2,2,256,128]{4,3,2,1,0:T(8,128)(2,1)}, u32[]{:S(2)}, u32[]{:S(2)}) %all-to-all-start) | async-done | bytes 4194336 | tf_op jit(solution)/shard_map/all_to_all | solution.py:92
  77.4 2.5 %copy.85 = bf16[16,2,2,256,128]{4,3,0,2,1:T(8,128)(2,1)S(1)} copy(bf16[16,2,2,256,128]{4,3,2,1,0:T(8,128)(2,1)} %all-to-all-done) | data formatting | bytes 8388608 | tf_op jit(solution)/shard_map/all_to_all | solution.py:92
  79.9 1.8 fusion.29
  81.7 0.8 copy-done.2
  82.5 4.1 %gather_fusion.2 = bf16[72,128,128]{2,1,0:T(8,128)(2,1)} fusion(bf16[64,128,128]{2,1,0:T(8,128)(2,1)} %bitcast.71, s32[1024]{0:T(1024)S(1)} %pad_clamp_fusion), kind=kCustom, calls=%fused_computation.1.clone | custom fusion | bytes 4718880 | tf_op jit(solution)/shard_map/jit(_take)/gather | solution.py:50
  86.5 2.5 %gather_fusion.3 = bf16[72,128,128]{2,1,0:T(8,128)(2,1)} fusion(bf16[64,128,128]{2,1,0:T(8,128)(2,1)S(1)} %bitcast.70, s32[1024]{0:T(1024)S(1)} %pad_clamp_fusion), kind=kCustom, calls=%fused_computation.3.clone | custom fusion | bytes 4718880 | tf_op jit(solution)/shard_map/jit(_take)/gather | solution.py:53
  89.0 2.9 %broadcast_select_fusion.1 = (bf16[72,128,128]{2,1,0:T(8,128)(2,1)S(1)}, bf16[72,128,128]{2,1,0:T(8,128)(2,1)S(1)}) fusion(bf16[72,128,128]{2,1,0:T(8,128)(2,1)} %gather_fusion.2, pred[72]{0:T(512)(128)(4,1)S(1)} %get-tuple-element.13, bf16[72,128,128]{2,1,0:T(8,128)(2,1)} %gather_fusion.3), kind=kLoop, calls=%fused_computation.20 | loop fusion | flops 2359296 | bytes 9437256 | tf_op jit(solution)/shard_map/jit(_take)/select_n | solution.py:50
  91.9 3.1 %fusion.34 = (f32[8,128]{1,0:T(8,128)S(1)}, f32[8,128,1152]{1,2,0:T(8,128)S(1)}) fusion(bf16[8,1152,128]{2,1,0:T(8,128)(2,1)S(1)} %bitcast.76, bf16[8,128,128]{2,1,0:T(8,128)(2,1)S(1)} %bitcast.82, pred[128,1152]{0,1:T(8,128)(4,1)S(1)} %bitcast_or_fusion, pred[8,1152]{1,0:T(8,128)(4,1)S(1)} %broadcast_bitcast_fusion), kind=kOutput, calls=%fused_computation.111 | convolution fusion | flops 306707456 | bytes 7500800 | tf_op jit(solution)/shard_map/zcs,zvs->zcv/dot_general | solution.py:56
  95.0 0.6 fusion.2
  95.7 1.3 fusion.19
  96.9 0.2 copy.83
  97.1 0.8 stack.19
  98.0 1.7 slice.48
  99.7 0.1 fusion.30
  99.8 2.5 %gather_fusion = bf16[72,128,128]{2,1,0:T(8,128)(2,1)} fusion(bf16[32,128,128]{2,1,0:T(8,128)(2,1)S(1)} %bitcast.69, s32[1024]{0:T(1024)S(1)} %pad_clamp_fusion.1), kind=kCustom, calls=%fused_computation.clone | custom fusion | bytes 4718880 | tf_op jit(solution)/shard_map/jit(_take)/gather | solution.py:50
  102.3 2.4 %gather_fusion.1 = bf16[72,128,128]{2,1,0:T(8,128)(2,1)} fusion(bf16[32,128,128]{2,1,0:T(8,128)(2,1)S(1)} %bitcast.68, s32[1024]{0:T(1024)S(1)} %pad_clamp_fusion.1), kind=kCustom, calls=%fused_computation.2.clone | custom fusion | bytes 4718880 | tf_op jit(solution)/shard_map/jit(_take)/gather | solution.py:53
  104.7 2.4 %broadcast_select_fusion.3 = (bf16[72,128,128]{2,1,0:T(8,128)(2,1)S(1)}, bf16[72,128,128]{2,1,0:T(8,128)(2,1)S(1)}) fusion(bf16[72,128,128]{2,1,0:T(8,128)(2,1)S(1)} %copy-done.3, pred[72]{0:T(512)(128)(4,1)S(1)} %get-tuple-element.57, bf16[72,128,128]{2,1,0:T(8,128)(2,1)} %gather_fusion.1), kind=kLoop, calls=%fused_computation.22 | loop fusion | flops 2359296 | bytes 9437256 | tf_op jit(solution)/shard_map/jit(_take)/select_n | solution.py:50
  107.1 2.9 %fusion.35 = (f32[8,128]{1,0:T(8,128)S(1)}, f32[8,128,1152]{1,2,0:T(8,128)S(1)}) fusion(bf16[8,1152,128]{2,1,0:T(8,128)(2,1)S(1)} %bitcast.75, bf16[8,128,128]{2,1,0:T(8,128)(2,1)S(1)} %bitcast.83, pred[128,1152]{0,1:T(8,128)(4,1)S(1)} %copy-done.8, pred[8,1152]{1,0:T(8,128)(4,1)S(1)} %broadcast_bitcast_fusion.1), kind=kOutput, calls=%fused_computation.112 | convolution fusion | flops 306707456 | bytes 7500800 | tf_op jit(solution)/shard_map/zcs,zvs->zcv/dot_general | solution.py:56
  110.1 0.6 fusion
  110.7 1.3 fusion.13
  112.0 0.2 copy.84
  112.4 10.2 %convolution_convert_fusion = bf16[512,8192]{1,0:T(8,128)(2,1)} fusion(bf16[512,512]{1,0:T(8,128)(2,1)S(1)} %bitcast.81, bf16[512,8192]{1,0:T(8,128)(2,1)} %param.14), kind=kOutput, calls=%fused_computation.4 | convolution fusion | flops 4299161600 | bytes 17301504 | tf_op jit(solution)/shard_map/dot_general | solution.py:126
  122.7 75.1 %reduce-scatter.2.cloned.1.call-done = bf16[32,8192]{1,0:T(8,128)(2,1)} async-done(((bf16[512,8192]{1,0:T(8,128)(2,1)}), bf16[32,8192]{1,0:T(8,128)(2,1)}) %reduce-scatter.2.cloned.1.call-update) | async-done | bytes 524304 | tf_op jit(solution)/shard_map/reduce_scatter | solution.py:125
  (72 shorter events, 3.0 us)
Async XLA Ops:
  6.5 11.8 %copy-start = (s32[64,4]{0,1:T(4,128)S(1)}, s32[64,4]{0,1:T(4,128)}, u32[]{:S(2)}) copy-start(s32[64,4]{0,1:T(4,128)} %param.17) | copy-start | bytes 3076
  10.6 7.7 %copy-start.10 = (s32[2,16]{1,0:T(2,128)S(1)}, s32[2,16]{1,0:T(2,128)}, u32[]{:S(2)}) copy-start(s32[2,16]{1,0:T(2,128)} %param.15) | copy-start | bytes 388
  10.6 9.8 %copy-start.9 = (s32[64,4]{0,1:T(4,128)S(1)}, s32[64,4]{0,1:T(4,128)}, u32[]{:S(2)}) copy-start(s32[64,4]{0,1:T(4,128)} %param.16) | copy-start | bytes 3076
  10.6 12.4 %copy-start.5 = (bf16[2,256,512]{2,1,0:T(8,128)(2,1)S(1)}, bf16[2,256,512]{2,1,0:T(8,128)(2,1)}, u32[]{:S(2)}) copy-start(bf16[2,256,512]{2,1,0:T(8,128)(2,1)} %param.11) | copy-start | bytes 1572868
  10.6 66.8 %all-to-all-start = ((bf16[16,2,2,256,128]{4,3,2,1,0:T(8,128)(2,1)}), bf16[16,2,2,256,128]{4,3,2,1,0:T(8,128)(2,1)}, u32[]{:S(2)}, u32[]{:S(2)}) async-start(bf16[16,2,2,256,128]{4,3,2,1,0:T(8,128)(2,1)} %stack.17), calls=%async_computation | async-start | bytes 8388608 | tf_op jit(solution)/shard_map/all_to_all | solution.py:92
  18.2 179.6 %reduce-scatter.2.cloned.1.call-start = ((), (), s32[]{:S(2)}) async-start(), calls=%async_computation.2 | async-start | bytes 8912896 | tf_op jit(solution)/shard_map/reduce_scatter | solution.py:125
  24.9 67.0 %copy-start.7 = (pred[128,1152]{0,1:T(8,128)(4,1)}, pred[128,1152]{0,1:T(8,128)(4,1)S(1)}, u32[]{:S(2)}) copy-start(pred[128,1152]{0,1:T(8,128)(4,1)S(1)} %bitcast_or_fusion) | copy-start | bytes 442372
  79.8 2.6 %copy-start.2 = (bf16[16,2,2,256,128]{4,3,0,2,1:T(8,128)(2,1)}, bf16[16,2,2,256,128]{4,3,0,2,1:T(8,128)(2,1)S(1)}, u32[]{:S(2)}) copy-start(bf16[16,2,2,256,128]{4,3,0,2,1:T(8,128)(2,1)S(1)} %copy.85) | copy-start | bytes 12582916
  102.3 2.4 %copy-start.3 = (bf16[72,128,128]{2,1,0:T(8,128)(2,1)S(1)}, bf16[72,128,128]{2,1,0:T(8,128)(2,1)}, u32[]{:S(2)}) copy-start(bf16[72,128,128]{2,1,0:T(8,128)(2,1)} %gather_fusion) | copy-start | bytes 7077892
  104.7 2.4 %copy-start.6 = (bf16[2,128,4,128]{3,1,0,2:T(8,128)(2,1)S(1)}, bf16[2,128,4,128]{3,1,0,2:T(8,128)(2,1)}, u32[]{:S(2)}) copy-start(bf16[2,128,4,128]{3,1,0,2:T(8,128)(2,1)} %copy.63) | copy-start | bytes 786436
  104.7 2.4 %copy-start.8 = (pred[128,1152]{0,1:T(8,128)(4,1)S(1)}, pred[128,1152]{0,1:T(8,128)(4,1)}, u32[]{:S(2)}) copy-start(pred[128,1152]{0,1:T(8,128)(4,1)} %copy-done.7) | copy-start | bytes 442372
  110.7 1.6 copy-start.4
  122.7 75.1 %copy-start.1 = (s32[64,4]{0,1:T(4,128)S(1)}, s32[64,4]{0,1:T(4,128)}, u32[]{:S(2)}) copy-start(s32[64,4]{0,1:T(4,128)} %param.17) | copy-start | bytes 3076
Sparse Core Ops, SparseCore 0:
  122.8 74.9 reduce-scatter.1
